TPU v7x, 256 devices: a whole 4x4x8 slice. The times are simulated.
256 devices in a mesh: wide: 64 (over y, z, core), narrow: 4 (over x).
Axes of the slice: x: 4, y: 4, z: 8, core: 2. Of those that a mesh axis runs over, the one named last changes fastest.
Arguments:
- patches: bfloat16 [65536, 1280], P('wide', 'narrow'), may hold values from -6 to 6
- norm_gain: float32 [1280], replicated, may hold values from 0.1 to 1.9
- norm_bias: float32 [1280], replicated, may hold values from -3 to 3
- w_in: bfloat16 [1280, 5120], P('wide', 'narrow'), may hold values from -0.15625 to 0.15625
- b_in: float32 [5120], P('narrow'), may hold values from -3 to 3
- w_out: bfloat16 [5120, 1280], P('narrow', 'wide'), may hold values from -0.078125 to 0.078125
- b_out: float32 [1280], P('narrow'), may hold values from -3 to 3
- w_proj: bfloat16 [4, 1280, 1280], P(None, 'narrow', 'wide'), may hold values from -0.078125 to 0.078125
- b_proj: float32 [1280], P('narrow'), may hold values from -3 to 3
- text: bfloat16 [32768, 1280], P('wide', 'narrow'), may hold values from -6 to 6
- place: int32 [16384], replicated, may hold values from -1 to 32767, as said below
Outputs:
- prompt_embeds: bfloat16 [32768, 1280], P('wide', 'narrow')
Inputs may be any that keep to these rules, and one draw needn't show every extreme that they name: `place`: of the 256 entries of one wide index (entries i * 256 to (i + 1) * 256 - 1), the valid ones (>= 0) come first and -1 fills the rest; three quarters or more are valid, and all are valid for some wide index. Valid values are distinct. For one wide index, at most 8 valid entries v have the same v // 512, and every wide index reaches 8 for some value.
All inputs are finite; a program needn't handle non-finite values.
Results may differ from a plain program's by a relative error of at most 0.012.
Values may be sent and summed in bfloat16 or wider, within the bound.
A program may use at most 64 MiB of HBM per device.

v0:
```python
import jax
import jax.numpy as jnp
from jax import lax
from jax.sharding import PartitionSpec as P


def select_rows(index, rows, count):
    pick = (jnp.arange(count, dtype=jnp.int32)[:, None] == index[None, :]).astype(rows.dtype)
    return jnp.dot(pick, rows, preferred_element_type=jnp.float32).astype(rows.dtype)


def per_device(
    patches, norm_gain, norm_bias, w_in, b_in, w_out, b_out, w_proj, b_proj, text, place
):
    groups = lax.axis_size("wide")
    width = w_in.shape[0]
    local = jnp.concatenate([w_in, w_out.T, w_proj.transpose(2, 0, 1).reshape(width, -1)], axis=0)
    gathered = lax.all_gather(local, "wide", axis=0, tiled=False)
    rows_in = gathered[:, :width].reshape(groups * width, -1)
    cols_out = gathered[:, width : 2 * width].reshape(groups * width, -1)
    proj_cols = gathered[:, 2 * width :].reshape(groups * width, -1)
    whole = lax.all_gather(patches, "narrow", axis=1, tiled=True)
    values = whole.astype(jnp.float32)
    center = jnp.mean(values, axis=-1, keepdims=True)
    spread = jnp.mean(jnp.square(values - center), axis=-1, keepdims=True)
    normed = ((values - center) * lax.rsqrt(spread + 1e-06) * norm_gain + norm_bias).astype(
        jnp.bfloat16
    )
    product = jnp.dot(normed, rows_in, preferred_element_type=jnp.float32)
    hidden = jax.nn.gelu(product + b_in, approximate=False).astype(jnp.bfloat16)
    partial_out = lax.dot_general(
        hidden, cols_out, (((1,), (1,)), ((), ())), preferred_element_type=jnp.float32
    )
    mlp_out = lax.psum_scatter(
        partial_out.astype(jnp.bfloat16), "narrow", scatter_dimension=1, tiled=True
    ).astype(jnp.float32)
    stream = (patches.astype(jnp.float32) + (mlp_out + b_out)).astype(jnp.bfloat16)
    merge_count = stream.shape[0] // 4
    merged = stream.reshape(merge_count, 4 * stream.shape[1])
    own_index = lax.axis_index("wide")
    seq_rows = text.shape[0]
    bucket = seq_rows // groups
    place_table = place.reshape(groups, merge_count)
    owners = jnp.where(place_table >= 0, place_table // seq_rows, groups)
    own_owners = lax.dynamic_index_in_dim(owners, own_index, 0, keepdims=False)
    owner_hits = (own_owners[:, None] == jnp.arange(groups, dtype=jnp.int32)[None, :]).astype(
        jnp.int32
    )
    slot_out = jnp.sum(jnp.cumsum(owner_hits, axis=0) * owner_hits, axis=1) - 1
    send_row = jnp.where(
        (own_owners < groups) & (slot_out < bucket), own_owners * bucket + slot_out, -1
    )
    arriving = owners == own_index
    slot_in = jnp.cumsum(arriving.astype(jnp.int32), axis=1) - 1
    slot_in = jnp.where(arriving, slot_in, bucket)
    local_row = place_table % seq_rows
    slot_hits = slot_in[:, :, None] == jnp.arange(bucket, dtype=jnp.int32)[None, None, :]
    targets = jnp.sum(jnp.where(slot_hits, local_row[:, :, None] + 1, 0), axis=1) - 1
    partial_proj = lax.dot_general(
        merged, proj_cols, (((1,), (1,)), ((), ())), preferred_element_type=jnp.float32
    )
    vision = (
        lax.psum_scatter(
            partial_proj.astype(jnp.bfloat16), "narrow", scatter_dimension=1, tiled=True
        ).astype(jnp.float32)
        + b_proj
    ).astype(jnp.bfloat16)
    outgoing = select_rows(send_row, vision, groups * bucket).reshape(groups, bucket, -1)
    received = lax.all_to_all(outgoing, "wide", split_axis=0, concat_axis=0, tiled=True)
    flat_targets = targets.reshape(-1)
    placed = select_rows(flat_targets, received.reshape(-1, received.shape[2]), seq_rows)
    hit = jnp.any(jnp.arange(seq_rows, dtype=jnp.int32)[:, None] == flat_targets[None, :], axis=1)
    return jnp.where(hit[:, None], placed, text)


def solution(mesh):
    placed = (
        P("wide", "narrow"),
        P(),
        P(),
        P("wide", "narrow"),
        P("narrow"),
        P("narrow", "wide"),
        P("narrow"),
        P(None, "narrow", "wide"),
        P("narrow"),
        P("wide", "narrow"),
        P(),
    )
    return jax.shard_map(
        per_device, mesh=mesh, in_specs=placed, out_specs=P("wide", "narrow"), check_vma=False
    )
```

profile of v0, /device:TPU:1, one launch (start us, length us, event | category | flops | bytes accessed | tf_op | source)
XLA Modules:
  0.0 286.6 jit_solution(14069685264983872683)
XLA Ops:
  6.5 0.0 all-gather.5.cloned.1.call-start
  6.5 0.7 all-gather.5.cloned.1.call-update
  7.3 0.0 all-gather.7.cloned.1.call-start
  7.3 0.9 reshape.177
  8.2 1.6 maximum_bitcast_fusion
  9.8 0.0 all-gather.7.cloned.1.call-update
  9.8 0.0 reduce-scatter.5.cloned.1.call-start
  9.9 40.8 %all-gather.5.cloned.1.call-done = bf16[1024,1280]{0,1:T(8,128)(2,1)} async-done(((bf16[1024,320]{0,1:T(8,128)(2,1)}), bf16[1024,1280]{0,1:T(8,128)(2,1)}) %all-gather.5.cloned.1.call-update) | async-done | bytes 2621456 | tf_op jit(solution)/shard_map/all_gather | solution.py:22
  50.7 2.2 convert_reduce_fusion
  52.9 2.5 fusion.2
  55.4 85.1 %all-gather.7.cloned.1.call-done = bf16[64,60,1280]{2,1,0:T(8,128)(2,1)} async-done(((bf16[1,60,1280]{2,1,0:T(8,128)(2,1)}), bf16[64,60,1280]{2,1,0:T(8,128)(2,1)}) %all-gather.7.cloned.1.call-update) | async-done | bytes 9830416 | tf_op jit(solution)/shard_map/all_gather | solution.py:18
  140.5 8.2 %fusion.72 = (bf16[64,20,1280]{2,1,0:T(8,128)(2,1)}, bf16[64,20,1280]{2,1,0:T(8,128)(2,1)}, bf16[64,20,1280]{2,1,0:T(8,128)(2,1)}) fusion(bf16[64,60,1280]{2,1,0:T(8,128)(2,1)} %all-gather.7.cloned.1.call-done), kind=kLoop, calls=%fused_computation.116 | loop fusion | bytes 19660800 | tf_op jit(solution)/shard_map/slice | solution.py:21
  148.7 6.1 %reshape.179 = bf16[1280,1280]{1,0:T(8,128)(2,1)} reshape(bf16[64,20,1280]{2,1,0:T(8,128)(2,1)} %get-tuple-element.6) | data formatting | bytes 6553600 | tf_op jit(solution)/shard_map/reshape | solution.py:20
  154.9 6.3 %reshape.178 = bf16[1280,1280]{1,0:T(8,128)(2,1)} reshape(bf16[64,20,1280]{2,1,0:T(8,128)(2,1)} %get-tuple-element.7) | data formatting | bytes 6553600 | tf_op jit(solution)/shard_map/reshape | solution.py:19
  161.2 0.0 copy-done
  161.2 0.0 copy-done.3
  161.2 0.0 copy-done.4
  161.2 0.0 copy-done.5
  161.2 0.0 copy-start.1
  161.2 21.5 %convolution_convert_fusion = bf16[1024,1280]{0,1:T(8,128)(2,1)} fusion(bf16[1280,1280]{1,0:T(8,128)(2,1)} %reshape.179, bf16[1280,1280]{1,0:T(8,128)(2,1)} %reshape.178, bf16[1024,1280]{0,1:T(8,128)(2,1)S(1)} %copy-done, f32[1280]{0:T(1024)S(1)} %copy-done.3, f32[1280]{0:T(1024)S(1)} %copy-done.4, f32[1280]{0:T(1024)S(1)} %copy-done.5, ...), kind=kOutput, calls=%fused_computation.27 | convolution fusion | flops 6806568960 | bytes 11820032 | tf_op jit(solution)/shard_map/dot_general | solution.py:31
  182.7 0.0 reduce-scatter.5.cloned.1.call-update
  182.7 0.0 reduce-scatter.7.cloned.1.call-start
  182.8 0.0 copy-done.1
  182.8 0.1 fusion.40
  182.9 0.6 reduce-window.14
  183.5 4.6 %reshape.181 = bf16[1280,1280]{1,0:T(8,128)(2,1)S(1)} reshape(bf16[64,20,1280]{2,1,0:T(8,128)(2,1)} %get-tuple-element.5) | data formatting | bytes 6553600 | tf_op jit(solution)/shard_map/reshape | solution.py:21
  188.1 27.8 %reduce-scatter.5.cloned.1.call-done = bf16[1024,320]{0,1:T(8,128)(2,1)} async-done(((bf16[1024,1280]{0,1:T(8,128)(2,1)}), bf16[1024,320]{0,1:T(8,128)(2,1)}) %reduce-scatter.5.cloned.1.call-update) | async-done | bytes 655376 | tf_op jit(solution)/shard_map/reduce_scatter | solution.py:34
  215.9 0.0 copy-done.2
  215.9 2.4 add_convert_fusion
  218.3 2.2 copy.38
  220.5 2.5 reshape.180
  223.0 3.0 %fusion.21 = bf16[1280,256]{1,0:T(8,128)(2,1)} fusion(bf16[256,1280]{1,0:T(8,128)(2,1)} %reshape.180, bf16[1280,1280]{1,0:T(8,128)(2,1)S(1)} %reshape.181), kind=kOutput, calls=%fused_computation.33 | convolution fusion | flops 839188480 | bytes 4587520 | tf_op jit(solution)/shard_map/dot_general | solution.py:59
  226.0 0.0 reduce-scatter.7.cloned.1.call-update
  226.0 0.2 slice_reduce_fusion.1
  226.3 0.1 fusion.30
  226.4 0.6 reduce-window.16
  227.0 0.2 slice_reduce_fusion
  227.2 0.1 fusion.36
  227.4 21.8 %reduce-scatter.7.cloned.1.call-done = bf16[320,256]{1,0:T(8,128)(2,1)} async-done(((bf16[1280,256]{1,0:T(8,128)(2,1)}), bf16[320,256]{1,0:T(8,128)(2,1)}) %reduce-scatter.7.cloned.1.call-update) | async-done | bytes 163856
  249.1 1.1 copy.42
  250.2 0.3 convolution_convert_fusion.2
  250.6 0.9 copy.40
  251.5 11.8 %all-to-all-start = ((bf16[64,8,320]{2,1,0:T(8,128)(2,1)}), bf16[64,8,320]{2,1,0:T(8,128)(2,1)S(1)}, u32[]{:S(2)}, u32[]{:S(2)}) async-start(bf16[64,8,320]{2,1,0:T(8,128)(2,1)} %bitcast.9), calls=%async_computation.1 | async-start | bytes 786432 | tf_op jit(solution)/shard_map/all_to_all | solution.py:69
  263.3 1.2 select_reduce_fusion
  264.5 0.1 sub.43
  264.6 0.2 fusion.25
  264.8 13.2 %all-to-all-done = bf16[64,8,320]{2,1,0:T(8,128)(2,1)S(1)} async-done(((bf16[64,8,320]{2,1,0:T(8,128)(2,1)}), bf16[64,8,320]{2,1,0:T(8,128)(2,1)S(1)}, u32[]{:S(2)}, u32[]{:S(2)}) %all-to-all-start) | async-done | bytes 327712 | tf_op jit(solution)/shard_map/all_to_all | solution.py:69
  277.9 2.1 fusion.24
  (19 shorter events, 0.2 us)
Async XLA Ops:
  6.5 44.2 %all-gather.5.cloned.1.call-start = ((), (), s32[]{:S(2)}) async-start(), calls=%async_computation.3 | async-start | bytes 3276800 | tf_op jit(solution)/shard_map/all_gather | solution.py:22
  7.3 133.2 %all-gather.7.cloned.1.call-start = ((), (), s32[]{:S(2)}) async-start(), calls=%async_computation.5 | async-start | bytes 10649600 | tf_op jit(solution)/shard_map/all_gather | solution.py:18
  9.8 206.1 %reduce-scatter.5.cloned.1.call-start = ((), (), s32[]{:S(2)}) async-start(), calls=%async_computation.4 | async-start | bytes 3276800 | tf_op jit(solution)/shard_map/reduce_scatter | solution.py:34
  154.9 6.3 %copy-start = (bf16[1024,1280]{0,1:T(8,128)(2,1)S(1)}, bf16[1024,1280]{0,1:T(8,128)(2,1)}, u32[]{:S(2)}) copy-start(bf16[1024,1280]{0,1:T(8,128)(2,1)} %all-gather.5.cloned.1.call-done) | copy-start | bytes 7864324
  154.9 6.3 %copy-start.3 = (f32[1280]{0:T(1024)S(1)}, f32[1280]{0:T(1024)}, u32[]{:S(2)}) copy-start(f32[1280]{0:T(1024)} %param.15) | copy-start | bytes 15364
  154.9 6.3 %copy-start.4 = (f32[1280]{0:T(1024)S(1)}, f32[1280]{0:T(1024)}, u32[]{:S(2)}) copy-start(f32[1280]{0:T(1024)} %param.13) | copy-start | bytes 15364
  154.9 6.3 %copy-start.5 = (f32[1280]{0:T(1024)S(1)}, f32[1280]{0:T(1024)}, u32[]{:S(2)}) copy-start(f32[1280]{0:T(1024)} %param.12) | copy-start | bytes 15364
  161.2 21.6 %copy-start.1 = (s32[16384]{0:T(1024)S(1)}, s32[16384]{0:T(1024)}, u32[]{:S(2)}) copy-start(s32[16384]{0:T(1024)} %param.21) | copy-start | bytes 196612
  182.7 33.2 %copy-start.2 = (f32[320]{0:T(512)S(1)}, f32[320]{0:T(512)}, u32[]{:S(2)}) copy-start(f32[320]{0:T(512)} %param.17) | copy-start | bytes 3844
  182.7 66.4 %reduce-scatter.7.cloned.1.call-start = ((), (), s32[]{:S(2)}) async-start(), calls=%async_computation.6 | async-start | bytes 819200
  218.3 31.9 %copy-start.6 = (f32[320]{0:T(512)S(1)}, f32[320]{0:T(512)}, u32[]{:S(2)}) copy-start(f32[320]{0:T(512)} %param.19) | copy-start | bytes 3844
  251.5 26.4 %all-to-all-start = ((bf16[64,8,320]{2,1,0:T(8,128)(2,1)}), bf16[64,8,320]{2,1,0:T(8,128)(2,1)S(1)}, u32[]{:S(2)}, u32[]{:S(2)}) async-start(bf16[64,8,320]{2,1,0:T(8,128)(2,1)} %bitcast.9), calls=%async_computation.1 | async-start | bytes 786432 | tf_op jit(solution)/shard_map/all_to_all | solution.py:69
Sparse Core Ops, SparseCore 0:
  9.2 41.5 all-gather.4
  53.5 86.9 all-gather.6
  182.8 33.0 reduce-scatter.4
  226.2 22.9 reduce-scatter.6
where the time goes:
time: 287 us
  waiting for transfers between devices  189 us (66%)
  local copies, waits for them, and re-layouts  33.5 us (12%)
  matrix products  26.9 us (9%)
  between operations  13.3 us (5%)
  starting transfers between devices  12 us (4%)
  other arithmetic  11.6 us (4%)
    all_gather x1, waiting for transfers between devices, per_device(): gathered = lax.all_gather(local, 'wide', axis=0, tiled=False)  85.1 us
    all_gather x1, waiting for transfers between devices, per_device(): whole = lax.all_gather(patches, 'narrow', axis=1, tiled=True)  40.8 us
    reduce_scatter x1, waiting for transfers between devices, per_device(): lax.psum_scatter(partial_out.astype(jnp.bfloat16), 'narrow', scatter_dime...  27.8 us
    unnamed x5, waiting for transfers between devices  22.5 us
    dot_general x1, matrix products, per_device(): lax.dot_general(hidden, cols_out, (((1,), (1,)), ((), ())), preferred_ele...  21.5 us
    all_to_all x1, waiting for transfers between devices, per_device(): lax.all_to_all(outgoing, 'wide', split_axis=0, concat_axis=0, tiled=True)  13.2 us
    all_to_all x1, starting transfers between devices, per_device(): lax.all_to_all(outgoing, 'wide', split_axis=0, concat_axis=0, tiled=True)  11.8 us
    slice x1, local copies, waits for them, and re-layouts, per_device(): proj_cols = gathered[:, 2 * width:].reshape(groups * width, -1)  8.25 us
  transfers between devices with their start and end apart: 5, of which 5 were waited for; matrix products, arithmetic and copies ran while one was open for 5% of the time, Pallas kernels for 0%

commit v1 on v0

--- a/solution.py
+++ b/solution.py
@@ -2,6 +2,16 @@
 import jax.numpy as jnp
 from jax import lax
 from jax.sharding import PartitionSpec as P
+
+
+def pass_along(shard, name, dim):
+    size = lax.axis_size(name)
+    held, tiles = (shard, [shard])
+    for _ in range(size - 1):
+        held = lax.ppermute(held, name, [(i, (i + 1) % size) for i in range(size)])
+        tiles.insert(0, held)
+    line = jnp.concatenate(tiles, axis=dim)
+    return jnp.roll(line, (lax.axis_index(name) + 1) * shard.shape[dim], axis=dim)
 
 
 def select_rows(index, rows, count):
@@ -19,7 +29,7 @@
     rows_in = gathered[:, :width].reshape(groups * width, -1)
     cols_out = gathered[:, width : 2 * width].reshape(groups * width, -1)
     proj_cols = gathered[:, 2 * width :].reshape(groups * width, -1)
-    whole = lax.all_gather(patches, "narrow", axis=1, tiled=True)
+    whole = pass_along(patches, "narrow", 1)
     values = whole.astype(jnp.float32)
     center = jnp.mean(values, axis=-1, keepdims=True)
     spread = jnp.mean(jnp.square(values - center), axis=-1, keepdims=True)

time: 287 us -> 243 us (0.85)
  waiting for transfers between devices: 189 us -> 143 us
  starting transfers between devices: 12 us -> 16.8 us
  other arithmetic: 11.6 us -> 7.7 us
    all_gather x1, waiting for transfers between devices: 85.1 us -> 41.5 us  [per_device(): gathered = lax.all_gather(local, 'wide', axis=0, tiled=False)]
    all_gather x1 -> x0, waiting for transfers between devices: 40.8 us -> none  [per_device(): whole = lax.all_gather(patches, 'narrow', axis=1, tiled=True)]
    ppermute x0 -> x3, waiting for transfers between devices: none -> 40.3 us  [pass_along(): held = lax.ppermute(held, name, [(i, (i + 1) % size) for i in range(size)])]
    ppermute x0 -> x3, starting transfers between devices: none -> 4.84 us  [pass_along(): held = lax.ppermute(held, name, [(i, (i + 1) % size) for i in range(size)])]
    unnamed x15 -> x26, local copies, waits for them, and re-layouts: 1.11 us -> 4.08 us
    unnamed x5 -> x4, waiting for transfers between devices: 22.5 us -> 21.7 us
  transfers between devices with their start and end apart: 5 -> 7, of which waited for: 5 -> 7; matrix products, arithmetic and copies ran while one was open for 5% -> 5% of each run, Pallas kernels for 0% -> 0%
where the time goes in v1:
time: 243 us
  waiting for transfers between devices  143 us (59%)
  local copies, waits for them, and re-layouts  34.2 us (14%)
  matrix products  27.6 us (11%)
  starting transfers between devices  16.8 us (7%)
  between operations  13.4 us (6%)
  other arithmetic  7.7 us (3%)
    all_gather x1, waiting for transfers between devices, per_device(): gathered = lax.all_gather(local, 'wide', axis=0, tiled=False)  41.5 us
    ppermute x3, waiting for transfers between devices, pass_along(): held = lax.ppermute(held, name, [(i, (i + 1) % size) for i in range(size)])  40.3 us
    reduce_scatter x1, waiting for transfers between devices, per_device(): lax.psum_scatter(partial_out.astype(jnp.bfloat16), 'narrow', scatter_dime...  26.3 us
    dot_general x1, matrix products, per_device(): lax.dot_general(hidden, cols_out, (((1,), (1,)), ((), ())), preferred_ele...  22.3 us
    unnamed x4, waiting for transfers between devices  21.7 us
    all_to_all x1, waiting for transfers between devices, per_device(): lax.all_to_all(outgoing, 'wide', split_axis=0, concat_axis=0, tiled=True)  13.2 us
    all_to_all x1, starting transfers between devices, per_device(): lax.all_to_all(outgoing, 'wide', split_axis=0, concat_axis=0, tiled=True)  11.9 us
    slice x1, local copies, waits for them, and re-layouts, per_device(): proj_cols = gathered[:, 2 * width:].reshape(groups * width, -1)  8.19 us
  transfers between devices with their start and end apart: 7, of which 7 were waited for; matrix products, arithmetic and copies ran while one was open for 5% of the time, Pallas kernels for 0%

profile of v1, /device:TPU:1, one launch (start us, length us, event | category | flops | bytes accessed | tf_op | source)
XLA Modules:
  0.0 242.7 jit_solution(12030579067904403789)
XLA Ops:
  6.5 1.0 reshape.177
  7.5 1.6 maximum_bitcast_fusion
  9.1 0.0 all-gather.4.cloned.1.call-update
  9.1 0.0 reduce-scatter.5.cloned.1.call-start
  9.2 2.1 collective-permute-start
  11.3 13.6 %collective-permute-done = bf16[1024,320]{0,1:T(8,128)(2,1)S(1)} collective-permute-done((bf16[1024,320]{0,1:T(8,128)(2,1)}, bf16[1024,320]{0,1:T(8,128)(2,1)S(1)}, u32[]{:S(2)}, u32[]{:S(2)}) %collective-permute-start) | collective-permute-done | bytes 655392 | tf_op jit(solution)/shard_map/ppermute | solution.py:11
  24.9 1.9 collective-permute-start.1
  26.8 13.7 %collective-permute-done.1 = bf16[1024,320]{0,1:T(8,128)(2,1)S(1)} collective-permute-done((bf16[1024,320]{0,1:T(8,128)(2,1)S(1)}, bf16[1024,320]{0,1:T(8,128)(2,1)S(1)}, u32[]{:S(2)}, u32[]{:S(2)}) %collective-permute-start.1) | collective-permute-done | bytes 655392 | tf_op jit(solution)/shard_map/ppermute | solution.py:11
  40.5 0.8 collective-permute-start.2
  41.3 13.0 %collective-permute-done.2 = bf16[1024,320]{0,1:T(8,128)(2,1)S(1)} collective-permute-done((bf16[1024,320]{0,1:T(8,128)(2,1)S(1)}, bf16[1024,320]{0,1:T(8,128)(2,1)S(1)}, u32[]{:S(2)}, u32[]{:S(2)}) %collective-permute-start.2) | collective-permute-done | bytes 655392 | tf_op jit(solution)/shard_map/ppermute | solution.py:11
  54.5 1.1 constant_dynamic-update-slice_fusion.4
  55.9 0.8 convert_reduce_fusion
  56.7 1.6 copy-done
  58.2 1.1 fusion.2
  59.3 41.5 %all-gather.4.cloned.1.call-done = bf16[64,60,1280]{2,1,0:T(8,128)(2,1)} async-done(((bf16[1,60,1280]{2,1,0:T(8,128)(2,1)}), bf16[64,60,1280]{2,1,0:T(8,128)(2,1)}) %all-gather.4.cloned.1.call-update) | async-done | bytes 9830416 | tf_op jit(solution)/shard_map/all_gather | solution.py:28
  100.8 8.2 %fusion.76 = (bf16[64,20,1280]{2,1,0:T(8,128)(2,1)}, bf16[64,20,1280]{2,1,0:T(8,128)(2,1)}, bf16[64,20,1280]{2,1,0:T(8,128)(2,1)}) fusion(bf16[64,60,1280]{2,1,0:T(8,128)(2,1)} %all-gather.4.cloned.1.call-done), kind=kLoop, calls=%fused_computation.126 | loop fusion | bytes 19660800 | tf_op jit(solution)/shard_map/slice | solution.py:31
  109.0 6.1 %reshape.179 = bf16[1280,1280]{1,0:T(8,128)(2,1)} reshape(bf16[64,20,1280]{2,1,0:T(8,128)(2,1)} %get-tuple-element.6) | data formatting | bytes 6553600 | tf_op jit(solution)/shard_map/reshape | solution.py:30
  115.1 6.2 %reshape.178 = bf16[1280,1280]{1,0:T(8,128)(2,1)} reshape(bf16[64,20,1280]{2,1,0:T(8,128)(2,1)} %get-tuple-element.7) | data formatting | bytes 6553600 | tf_op jit(solution)/shard_map/reshape | solution.py:29
  121.3 0.0 copy-start.2
  121.3 22.3 %convolution_convert_fusion = bf16[1024,1280]{0,1:T(8,128)(2,1)} fusion(bf16[1280,1280]{1,0:T(8,128)(2,1)} %reshape.179, bf16[1280,1280]{1,0:T(8,128)(2,1)} %reshape.178, f32[1280]{0:T(1024)S(1)} %copy-done.5, f32[1280]{0:T(1024)S(1)} %copy-done.6, f32[1280]{0:T(1024)S(1)} %copy-done.7, f32[1024]{0:T(1024)S(1)} %add_rsqrt_fusion, ...), kind=kOutput, calls=%fused_computation.27 | convolution fusion | flops 6806568960 | bytes 11820036 | tf_op jit(solution)/shard_map/dot_general | solution.py:41
  143.6 0.0 reduce-scatter.5.cloned.1.call-update
  143.6 0.0 reduce-scatter.7.cloned.1.call-start
  143.7 0.1 fusion.42
  143.8 0.6 reduce-window.14
  144.4 6.1 %reshape.181 = bf16[1280,1280]{1,0:T(8,128)(2,1)} reshape(bf16[64,20,1280]{2,1,0:T(8,128)(2,1)} %get-tuple-element.5) | data formatting | bytes 6553600 | tf_op jit(solution)/shard_map/reshape | solution.py:31
  150.5 26.3 %reduce-scatter.5.cloned.1.call-done = bf16[1024,320]{0,1:T(8,128)(2,1)} async-done(((bf16[1024,1280]{0,1:T(8,128)(2,1)}), bf16[1024,320]{0,1:T(8,128)(2,1)}) %reduce-scatter.5.cloned.1.call-update) | async-done | bytes 655376 | tf_op jit(solution)/shard_map/reduce_scatter | solution.py:44
  176.8 1.3 add_convert_fusion
  178.2 0.0 copy-start.8
  178.2 0.4 copy.38
  178.6 0.0 copy-start.4
  178.6 0.7 reshape.180
  179.3 3.8 %fusion.21 = bf16[1280,256]{1,0:T(8,128)(2,1)} fusion(bf16[256,1280]{1,0:T(8,128)(2,1)S(1)} %reshape.180, bf16[1280,1280]{1,0:T(8,128)(2,1)} %reshape.181), kind=kOutput, calls=%fused_computation.33 | convolution fusion | flops 839188480 | bytes 4587520 | tf_op jit(solution)/shard_map/dot_general | solution.py:69
  183.1 0.0 reduce-scatter.7.cloned.1.call-update
  183.1 0.2 slice_reduce_fusion.1
  183.3 0.1 fusion.32
  183.5 0.6 reduce-window.16
  184.1 0.2 slice_reduce_fusion
  184.3 0.1 fusion.38
  184.5 21.7 %reduce-scatter.7.cloned.1.call-done = bf16[320,256]{1,0:T(8,128)(2,1)} async-done(((bf16[1280,256]{1,0:T(8,128)(2,1)}), bf16[320,256]{1,0:T(8,128)(2,1)}) %reduce-scatter.7.cloned.1.call-update) | async-done | bytes 163856
  206.2 1.1 copy.42
  207.3 0.3 convolution_convert_fusion.2
  207.6 0.9 copy.40
  208.5 11.9 %all-to-all-start = ((bf16[64,8,320]{2,1,0:T(8,128)(2,1)}), bf16[64,8,320]{2,1,0:T(8,128)(2,1)S(1)}, u32[]{:S(2)}, u32[]{:S(2)}) async-start(bf16[64,8,320]{2,1,0:T(8,128)(2,1)} %bitcast.9), calls=%async_computation.1 | async-start | bytes 786432 | tf_op jit(solution)/shard_map/all_to_all | solution.py:79
  220.4 1.2 select_reduce_fusion
  221.6 0.1 sub.47
  221.7 0.2 fusion.27
  221.8 13.2 %all-to-all-done = bf16[64,8,320]{2,1,0:T(8,128)(2,1)S(1)} async-done(((bf16[64,8,320]{2,1,0:T(8,128)(2,1)}), bf16[64,8,320]{2,1,0:T(8,128)(2,1)S(1)}, u32[]{:S(2)}, u32[]{:S(2)}) %all-to-all-start) | async-done | bytes 327712 | tf_op jit(solution)/shard_map/all_to_all | solution.py:79
  235.0 1.2 fusion.26
  (34 shorter events, 0.5 us)
Async XLA Ops:
  6.5 49.2 %copy-start.1 = (bf16[1024,320]{0,1:T(8,128)(2,1)S(1)}, bf16[1024,320]{0,1:T(8,128)(2,1)}, u32[]{:S(2)}) copy-start(bf16[1024,320]{0,1:T(8,128)(2,1)} %param.11) | copy-start | bytes 1966084
  6.5 94.3 %all-gather.4.cloned.1.call-start = ((), (), s32[]{:S(2)}) async-start(), calls=%async_computation.4 | async-start | bytes 10649600 | tf_op jit(solution)/shard_map/all_gather | solution.py:28
  9.1 167.7 %reduce-scatter.5.cloned.1.call-start = ((), (), s32[]{:S(2)}) async-start(), calls=%async_computation.3 | async-start | bytes 3276800 | tf_op jit(solution)/shard_map/reduce_scatter | solution.py:44
  9.2 15.8 %collective-permute-start = (bf16[1024,320]{0,1:T(8,128)(2,1)}, bf16[1024,320]{0,1:T(8,128)(2,1)S(1)}, u32[]{:S(2)}, u32[]{:S(2)}) collective-permute-start(bf16[1024,320]{0,1:T(8,128)(2,1)} %param.11), channel_id=1, source_target_pairs={{0,1},{1,2},{2,3},{3,0},{4,5},{5,6},{6,7},{7,4},{8,9},{9,10},{10,1... | collective-permute-start | bytes 1966088 | tf_op jit(solution)/shard_map/ppermute | solution.py:11
  24.9 15.5 %collective-permute-start.1 = (bf16[1024,320]{0,1:T(8,128)(2,1)S(1)}, bf16[1024,320]{0,1:T(8,128)(2,1)S(1)}, u32[]{:S(2)}, u32[]{:S(2)}) collective-permute-start(bf16[1024,320]{0,1:T(8,128)(2,1)S(1)} %collective-permute-done), channel_id=1, source_target_pairs={{0,1},{1,2},{2,3},{3,0},{4,5},{5,6},{6,7},{7,4},{8,9},{9,10},{10,1... | collective-permute-start | bytes 1966088 | tf_op jit(solution)/shard_map/ppermute | solution.py:11
  40.5 13.9 %collective-permute-start.2 = (bf16[1024,320]{0,1:T(8,128)(2,1)S(1)}, bf16[1024,320]{0,1:T(8,128)(2,1)S(1)}, u32[]{:S(2)}, u32[]{:S(2)}) collective-permute-start(bf16[1024,320]{0,1:T(8,128)(2,1)S(1)} %collective-permute-done.1), channel_id=1, source_target_pairs={{0,1},{1,2},{2,3},{3,0},{4,5},{5,6},{6,7},{7,4},{8,9},{9,10},{10,1... | collective-permute-start | bytes 1966088 | tf_op jit(solution)/shard_map/ppermute | solution.py:11
  55.8 2.4 copy-start
  115.1 6.2 %copy-start.5 = (f32[1280]{0:T(1024)S(1)}, f32[1280]{0:T(1024)}, u32[]{:S(2)}) copy-start(f32[1280]{0:T(1024)} %param.15) | copy-start | bytes 15364
  115.1 6.2 %copy-start.6 = (f32[1280]{0:T(1024)S(1)}, f32[1280]{0:T(1024)}, u32[]{:S(2)}) copy-start(f32[1280]{0:T(1024)} %param.13) | copy-start | bytes 15364
  115.1 6.2 %copy-start.7 = (f32[1280]{0:T(1024)S(1)}, f32[1280]{0:T(1024)}, u32[]{:S(2)}) copy-start(f32[1280]{0:T(1024)} %param.12) | copy-start | bytes 15364
  121.3 22.4 %copy-start.2 = (s32[16384]{0:T(1024)S(1)}, s32[16384]{0:T(1024)}, u32[]{:S(2)}) copy-start(s32[16384]{0:T(1024)} %param.21) | copy-start | bytes 196612
  143.6 33.2 %copy-start.3 = (f32[320]{0:T(512)S(1)}, f32[320]{0:T(512)}, u32[]{:S(2)}) copy-start(f32[320]{0:T(512)} %param.17) | copy-start | bytes 3844
  143.6 62.5 %reduce-scatter.7.cloned.1.call-start = ((), (), s32[]{:S(2)}) async-start(), calls=%async_computation.5 | async-start | bytes 819200
  178.2 29.1 %copy-start.8 = (f32[320]{0:T(512)S(1)}, f32[320]{0:T(512)}, u32[]{:S(2)}) copy-start(f32[320]{0:T(512)} %param.19) | copy-start | bytes 3844
  178.6 56.4 %copy-start.4 = (bf16[512,320]{0,1:T(8,128)(2,1)S(1)}, bf16[512,320]{0,1:T(8,128)(2,1)}, u32[]{:S(2)}) copy-start(bf16[512,320]{0,1:T(8,128)(2,1)} %param.20) | copy-start | bytes 983044
  208.5 26.5 %all-to-all-start = ((bf16[64,8,320]{2,1,0:T(8,128)(2,1)}), bf16[64,8,320]{2,1,0:T(8,128)(2,1)S(1)}, u32[]{:S(2)}, u32[]{:S(2)}) async-start(bf16[64,8,320]{2,1,0:T(8,128)(2,1)} %bitcast.9), calls=%async_computation.1 | async-start | bytes 786432 | tf_op jit(solution)/shard_map/all_to_all | solution.py:79
Sparse Core Ops, SparseCore 0:
  10.1 90.6 all-gather.3
  143.8 33.0 reduce-scatter.4
  183.2 22.8 reduce-scatter.6
